TPU v7x, 128 devices: a whole 4x4x4 slice. The times are simulated.
128 devices in a mesh: query: 4 (over z_lo, core), lib: 32 (over x, y, z_hi).
Axes of the slice: x: 4, y: 4, z: 4 (z_hi: 2, z_lo: 2; z = z_hi * 2 + z_lo), core: 2. Of those that a mesh axis runs over, the one named last changes fastest.
Arguments:
- queries: bfloat16 [4096, 2048], P(('query', 'lib')), may hold values from -64 to 64
- query_bucket: int32 [4096], P(('query', 'lib')), may hold values from 0 to 63, as said below
- library: bfloat16 [98304, 2048], P(('lib', 'query')), may hold values from -64 to 64
- library_time: bfloat16 [98304], P(('lib', 'query')), may hold values from 0 to 2
- library_bucket: int32 [98304], P(('lib', 'query')), may hold values from 0 to 63, as said below
Outputs:
- expected_spectra: bfloat16 [4096, 2048], P(('query', 'lib'))
- expected_time: float32 [4096], P(('query', 'lib'))
- log_evidence: float32 [4096], P(('query', 'lib'))
Inputs may be any that keep to these rules, and one draw needn't show every extreme that they name: `query_bucket`: library entries whose bucket differs from a query's by at most one are that query's candidates; the queries held by the devices at index i of lib lie in buckets 2 i and 2 i + 1. `library_bucket`: the library entries of every device hold each of the 64 buckets exactly 3072 // 256 times.
All inputs are finite; a program needn't handle non-finite values.
Results may differ from a plain program's by a relative error of at most 0.003.
Values may be sent and summed in bfloat16 or wider, within the bound.
A program may use at most 128 MiB of HBM per device.

v0:
```python
import jax
import jax.numpy as jnp
from jax import lax
from jax.sharding import PartitionSpec as P

SHARPNESS = 448


def entry_scale(spectra_rows):
    return lax.rsqrt(jnp.mean(jnp.square(spectra_rows.astype(jnp.float32)), axis=1) + 1e-06)


def scaled_scores(query_block, query_scale, block_bucket, entries, entry_bucket):
    products = lax.dot_general(
        query_block, entries, (((1,), (1,)), ((), ())), preferred_element_type=jnp.float32
    )
    inside = jnp.abs(block_bucket[:, None] - entry_bucket[None, :]) <= 1
    return jnp.where(
        inside, products * query_scale[:, None] * entry_scale(entries)[None, :], -jnp.inf
    )


def finish(spectra_sum, totals, time_sum, own_maxima):
    expected = (spectra_sum / totals[:, None]).astype(jnp.bfloat16)
    return (expected, time_sum / totals, own_maxima + jnp.log(totals))


def per_device(queries, query_bucket, library, library_time, library_bucket):
    own_rows = queries.shape[0]
    bin_count = queries.shape[1]
    query_block, block_bucket = (
        lax.all_gather(queries, "lib", axis=0, tiled=True),
        lax.all_gather(query_bucket, "lib", axis=0, tiled=True),
    )
    query_scale = entry_scale(query_block) * (SHARPNESS / bin_count)
    entries, entry_time, entry_bucket = (
        lax.all_gather(library, "query", axis=0, tiled=True),
        lax.all_gather(library_time, "query", axis=0, tiled=True),
        lax.all_gather(library_bucket, "query", axis=0, tiled=True),
    )
    scores = scaled_scores(query_block, query_scale, block_bucket, entries, entry_bucket)
    maxima = lax.pmax(jnp.max(scores, axis=1), "lib")
    weights = jnp.exp(scores - maxima[:, None]).astype(jnp.bfloat16)
    total_part = jnp.sum(weights.astype(jnp.float32), axis=1)
    spectra_part = jnp.dot(weights, entries, preferred_element_type=jnp.float32)
    time_part = jnp.dot(weights, entry_time, preferred_element_type=jnp.float32)
    first_row = lax.axis_index("lib") * own_rows
    total_all, time_all = lax.psum((total_part, time_part), "lib")
    spectra_sum = lax.psum_scatter(spectra_part, "lib", scatter_dimension=0, tiled=True)
    totals = lax.dynamic_slice_in_dim(total_all, first_row, own_rows)
    time_sum = lax.dynamic_slice_in_dim(time_all, first_row, own_rows)
    own_maxima = lax.dynamic_slice_in_dim(maxima, first_row, own_rows)
    return finish(spectra_sum, totals, time_sum, own_maxima)


def solution(mesh):
    placed = (
        P(("query", "lib"), None),
        P(("query", "lib")),
        P(("lib", "query"), None),
        P(("lib", "query")),
        P(("lib", "query")),
    )
    return jax.shard_map(
        per_device,
        mesh=mesh,
        in_specs=placed,
        out_specs=(P(("query", "lib"), None), P(("query", "lib")), P(("query", "lib"))),
        check_vma=False,
    )
```

profile of v0, /device:TPU:0, one launch (start us, length us, event | category | flops | bytes accessed | tf_op | source)
XLA Modules:
  0.0 572.3 jit_solution(1006789328680344113)
XLA Ops:
  7.2 0.0 all-gather.5.cloned.1.call-start
  7.2 0.7 all-gather.5.cloned.1.call-update
  7.9 0.0 all-gather.7.cloned.1.call-start
  7.9 0.7 all-gather.7.cloned.1.call-update
  8.6 0.0 reduce-scatter.2.cloned.1.call-start
  8.7 0.7 reshape.24
  9.4 1.2 dynamic-slice
  11.3 0.9 dynamic-update-slice
  12.2 21.3 %all-reduce = s32[1024]{0:T(1024)S(1)} all-reduce(s32[1024]{0:T(1024)S(1)} %dynamic-update-slice), channel_id=1, replica_groups=mesh['query'=4,'lib'=32] {'lib'}, use_global_device_ids=true, to_apply=%add | all-reduce | flops 1024 | bytes 8192
  33.5 5.2 all-gather
  38.7 57.0 %all-gather.5.cloned.1.call-done = bf16[1024,2048]{1,0:T(8,128)(2,1)} async-done(((bf16[32,2048]{1,0:T(8,128)(2,1)}), bf16[1024,2048]{1,0:T(8,128)(2,1)}) %all-gather.5.cloned.1.call-update) | async-done | bytes 4194320 | tf_op jit(solution)/shard_map/all_gather | solution.py:32
  95.7 3.1 multiply_reduce_fusion.1
  98.8 109.7 %all-gather.7.cloned.1.call-done = bf16[3072,2048]{1,0:T(8,128)(2,1)} async-done(((bf16[768,2048]{1,0:T(8,128)(2,1)}), bf16[3072,2048]{1,0:T(8,128)(2,1)}) %all-gather.7.cloned.1.call-update) | async-done | bytes 12582928 | tf_op jit(solution)/shard_map/all_gather | solution.py:37
  208.4 0.0 copy-start.1
  208.4 7.2 %multiply_reduce_fusion = f32[3072]{0:T(1024)S(1)} fusion(bf16[3072,2048]{1,0:T(8,128)(2,1)} %all-gather.7.cloned.1.call-done), kind=kLoop, calls=%fused_computation | loop fusion | flops 18871296 | bytes 12595200 | tf_op jit(solution)/shard_map/reduce_sum | solution.py:10
  215.7 0.0 copy-done.1
  215.7 19.3 %fusion = (f32[1024]{0:T(1024)S(1)}, f32[1024,3072]{1,0:T(8,128)}) fusion(f32[3072]{0:T(1024)S(1)} %add_rsqrt_fusion, f32[1024]{0:T(1024)S(1)} %rsqrt_multiply_fusion, s32[3072]{0:T(1024)S(1)} %bitcast.10, s32[1024]{0:T(1024)S(1)} %all-reduce, bf16[1024,2048]{1,0:T(8,128)(2,1)S(1)} %copy-done.1, bf16[3072,2048]{1,0:T(8,128)(2,1)} %all-gather.7.cloned.1.call-done), kind=kOutput, calls=%fused_computation.6 | convolution fusion | flops 12906920960 | bytes 29396992 | tf_op jit(solution)/shard_map/dot_general | solution.py:14
  235.0 96.7 %pmax.7 = f32[1024]{0:T(1024)S(1)} all-reduce(f32[1024]{0:T(1024)S(1)} %get-tuple-element.9), channel_id=1, replica_groups=mesh['query'=4,'lib'=32] {'lib'}, use_global_device_ids=true, to_apply=%region_3.4 | all-reduce | flops 1024 | bytes 8192 | tf_op jit(solution)/shard_map/pmax | solution.py:42
  331.7 8.3 %convert_reduce_fusion = (f32[1024]{0:T(1024)S(1)}, bf16[1024,3072]{1,0:T(8,128)(2,1)S(1)}) fusion(f32[1024]{0:T(1024)S(1)} %pmax.7, f32[3072]{0:T(1024)S(1)} %add_rsqrt_fusion, f32[1024,3072]{1,0:T(8,128)} %get-tuple-element.10, f32[1024]{0:T(1024)S(1)} %rsqrt_multiply_fusion, s32[3072]{0:T(1024)S(1)} %bitcast.11, s32[1024]{0:T(1024)S(1)} %all-reduce), kind=kLoop, calls=%fused_computation.1 | loop fusion | flops 31456256 | bytes 18915328 | tf_op jit(solution)/shard_map/reduce_sum | solution.py:44
  339.9 0.0 copy-start
  340.0 2.7 copy-done
  342.6 0.0 copy-start.2
  342.6 16.9 %fusion.1 = f32[1024,2048]{1,0:T(8,128)} fusion(bf16[1024,3072]{1,0:T(8,128)(2,1)S(1)} %get-tuple-element.8, bf16[3072,2048]{1,0:T(8,128)(2,1)} %all-gather.7.cloned.1.call-done), kind=kOutput, calls=%fused_computation.12 | convolution fusion | flops 12884901888 | bytes 27262976 | tf_op jit(solution)/shard_map/dot_general | solution.py:45
  359.5 0.0 reduce-scatter.2.cloned.1.call-update
  359.6 0.0 copy-done.2
  359.6 5.2 all-gather.1
  364.8 4.5 fusion.2
  369.3 90.5 %all-reduce.1 = (f32[1024]{0:T(1024)S(1)}, f32[1024]{0:T(1024)S(1)}) all-reduce(f32[1024]{0:T(1024)S(1)} %get-tuple-element.7, f32[1024]{0:T(1024)S(1)} %bitcast.13), channel_id=1, replica_groups=mesh['query'=4,'lib'=32] {'lib'}, use_global_device_ids=true, to_apply=%region_6.7 | all-reduce | flops 2048 | bytes 16384 | tf_op jit(solution)/shard_map/psum | solution.py:48
  459.8 0.6 log_add_fusion
  460.4 0.6 dynamic-slice_divide_fusion
  461.0 103.1 %reduce-scatter.2.cloned.1.call-done = f32[32,2048]{1,0:T(8,128)} async-done(((f32[1024,2048]{1,0:T(8,128)}), f32[32,2048]{1,0:T(8,128)}) %reduce-scatter.2.cloned.1.call-update) | async-done | bytes 262160 | tf_op jit(solution)/shard_map/reduce_scatter | solution.py:49
  564.1 1.7 divide_convert_fusion
  (4 shorter events, 0.0 us)
Async XLA Ops:
  7.2 88.5 %all-gather.5.cloned.1.call-start = ((), (), s32[]{:S(2)}) async-start(), calls=%async_computation.1 | async-start | bytes 4325376 | tf_op jit(solution)/shard_map/all_gather | solution.py:32
  7.9 200.5 %all-gather.7.cloned.1.call-start = ((), (), s32[]{:S(2)}) async-start(), calls=%async_computation.2 | async-start | bytes 15728640 | tf_op jit(solution)/shard_map/all_gather | solution.py:37
  8.6 555.5 %reduce-scatter.2.cloned.1.call-start = ((), (), s32[]{:S(2)}) async-start(), calls=%async_computation.3 | async-start | bytes 8650752 | tf_op jit(solution)/shard_map/reduce_scatter | solution.py:49
  208.4 7.3 %copy-start.1 = (bf16[1024,2048]{1,0:T(8,128)(2,1)S(1)}, bf16[1024,2048]{1,0:T(8,128)(2,1)}, u32[]{:S(2)}) copy-start(bf16[1024,2048]{1,0:T(8,128)(2,1)} %all-gather.5.cloned.1.call-done) | copy-start | bytes 12582916
  339.9 2.7 copy-start
  342.6 17.0 %copy-start.2 = (bf16[768]{0:T(1024)(128)(2,1)S(1)}, bf16[768]{0:T(1024)(128)(2,1)}, u32[]{:S(2)}) copy-start(bf16[768]{0:T(1024)(128)(2,1)} %param.8) | copy-start | bytes 4612
Sparse Core Ops, SparseCore 0:
  11.0 84.6 all-gather.4
  97.4 111.0 all-gather.6
  359.7 204.3 reduce-scatter.1
where the time goes:
time: 573 us; the launch traced here: 572 us
  waiting for transfers between devices  271 us (47%)
  blocking collectives  219 us (38%)
  matrix products  40.7 us (7%)
  other arithmetic  21.5 us (4%)
  between operations  14.5 us (3%)
    all_gather x1, waiting for transfers between devices, per_device(): lax.all_gather(library, 'query', axis=0, tiled=True)  110 us
    reduce_scatter x1, waiting for transfers between devices, per_device(): lax.psum_scatter(spectra_part, 'lib', scatter_dimension=0, tiled=True)  103 us
    pmax x1, blocking collectives, per_device(): maxima = lax.pmax(jnp.max(scores, axis=1), 'lib')  96.7 us
    psum x1, blocking collectives, per_device(): total_all, time_all = lax.psum((total_part, time_part), 'lib')  90.5 us
    all_gather x1, waiting for transfers between devices, per_device(): lax.all_gather(queries, 'lib', axis=0, tiled=True)  57 us
    unnamed x1, blocking collectives  21.3 us
    dot_general x1, matrix products, scaled_scores(): lax.dot_general(query_block, entries, (((1,), (1,)), ((), ())), preferred...  19.3 us
    dot_general x1, matrix products, per_device(): spectra_part = jnp.dot(weights, entries, preferred_element_type=jnp.float32)  16.9 us
  transfers between devices with their start and end apart: 3, of which 3 were waited for; matrix products, arithmetic and copies ran while one was open for 2% of the time, Pallas kernels for 0%

commit v1 on v0

v1 whole, which is shorter than its diff:
```python
import jax
import jax.numpy as jnp
from jax import lax
from jax.sharding import PartitionSpec as P

SHARPNESS = 448
PER_BUCKET = 12
N_LIB = 32


def entry_scale(spectra_rows):
    return lax.rsqrt(jnp.mean(jnp.square(spectra_rows.astype(jnp.float32)), axis=1) + 1e-06)


def bucket_positions(bucket):
    n = bucket.shape[0]
    at = jnp.arange(n)
    same = (bucket[None, :] == bucket[:, None]) & (at[None, :] < at[:, None])
    rank = jnp.sum(same.astype(jnp.int32), axis=1)
    return bucket * PER_BUCKET + rank


def per_device(queries, query_bucket, library, library_time, library_bucket):
    own_rows, bin_count = queries.shape
    lib_at = lax.axis_index("lib")
    positions = bucket_positions(library_bucket)
    row = jnp.arange(N_LIB * 48)
    wanted = (row // 48) * 24 - 12 + row % 48
    pick = (wanted[:, None] == positions[None, :]).astype(jnp.bfloat16)
    send = jnp.dot(pick, library, preferred_element_type=jnp.float32).astype(jnp.bfloat16)
    send_time = jnp.dot(pick, library_time, preferred_element_type=jnp.float32).astype(jnp.bfloat16)
    entries = lax.all_to_all(send.reshape(N_LIB, 48, bin_count), "lib", 0, 0).reshape(N_LIB * 48, bin_count)
    entry_time = lax.all_to_all(send_time.reshape(N_LIB, 48), "lib", 0, 0).reshape(N_LIB * 48)
    query_block = lax.all_gather(queries, "query", axis=0, tiled=True)
    block_bucket = lax.all_gather(query_bucket, "query", axis=0, tiled=True)
    query_scale = entry_scale(query_block) * (SHARPNESS / bin_count)
    products = lax.dot_general(query_block, entries, (((1,), (1,)), ((), ())), preferred_element_type=jnp.float32)
    row_bucket = 2 * lib_at - 1 + (row % 48) // PER_BUCKET
    inside = jnp.abs(block_bucket[:, None] - row_bucket[None, :]) <= 1
    inside = inside & (row_bucket >= 0)[None, :] & (row_bucket < 2 * N_LIB)[None, :]
    scores = jnp.where(inside, products * query_scale[:, None] * entry_scale(entries)[None, :], -jnp.inf)
    maxima = lax.pmax(jnp.max(scores, axis=1), "query")
    weights = jnp.exp(scores - maxima[:, None]).astype(jnp.bfloat16)
    total_part = jnp.sum(weights.astype(jnp.float32), axis=1)
    spectra_part = jnp.dot(weights, entries, preferred_element_type=jnp.float32)
    time_part = jnp.dot(weights, entry_time, preferred_element_type=jnp.float32)
    total_all, time_all = lax.psum((total_part, time_part), "query")
    spectra_sum = lax.psum_scatter(spectra_part, "query", scatter_dimension=0, tiled=True)
    first_row = lax.axis_index("query") * own_rows
    totals = lax.dynamic_slice_in_dim(total_all, first_row, own_rows)
    time_sum = lax.dynamic_slice_in_dim(time_all, first_row, own_rows)
    own_maxima = lax.dynamic_slice_in_dim(maxima, first_row, own_rows)
    expected = (spectra_sum / totals[:, None]).astype(jnp.bfloat16)
    return (expected, time_sum / totals, own_maxima + jnp.log(totals))


def solution(mesh):
    placed = (
        P(("query", "lib"), None),
        P(("query", "lib")),
        P(("lib", "query"), None),
        P(("lib", "query")),
        P(("lib", "query")),
    )
    return jax.shard_map(
        per_device,
        mesh=mesh,
        in_specs=placed,
        out_specs=(P(("query", "lib"), None), P(("query", "lib")), P(("query", "lib"))),
        check_vma=False,
    )
```

time: 573 us -> 189 us (0.33)
  waiting for transfers between devices: 271 us -> 68 us
  blocking collectives: 219 us -> 52.7 us
  matrix products: 40.7 us -> 18 us
  starting transfers between devices: 0.11 us -> 18.2 us
  other arithmetic: 21.5 us -> 12.3 us
    all_gather x2 -> x0, waiting for transfers between devices: 167 us -> none  [the longest x1 110 us: per_device(): lax.all_gather(library, 'query', axis=0, tiled=True)]
    reduce_scatter x1, waiting for transfers between devices: 103 us -> 0.01 us  [per_device(): lax.psum_scatter(spectra_part, 'query', scatter_dimension=0, tiled=True)]
    pmax x1, blocking collectives: 96.7 us -> 5.63 us  [per_device(): maxima = lax.pmax(jnp.max(scores, axis=1), 'query')]
    psum x1, blocking collectives: 90.5 us -> 5.78 us  [per_device(): total_all, time_all = lax.psum((total_part, time_part), 'query')]
    all_to_all x0 -> x2, waiting for transfers between devices: none -> 68 us  [the longest x1 58.3 us: per_device(): lax.all_to_all(send.reshape(N_LIB, 48, bin_count), 'lib', 0, 0)]
    all_to_all x0 -> x2, starting transfers between devices: none -> 18.1 us  [the longest x1 11 us: per_device(): lax.all_to_all(send.reshape(N_LIB, 48, bin_count), 'lib', 0, 0)]
    dot_general x1, matrix products: 16.9 us -> 4.8 us  [per_device(): spectra_part = jnp.dot(weights, entries, preferred_element_type=jnp.float32)]
    reduce_sum x1, other arithmetic: 8.25 us -> 1.87 us  [per_device(): total_part = jnp.sum(weights.astype(jnp.float32), axis=1)]
  transfers between devices with their start and end apart: 3 -> 3, of which waited for: 3 -> 2; matrix products, arithmetic and copies ran while one was open for 2% -> 3% of each run, Pallas kernels for 0% -> 0%
where the time goes in v1:
time: 189 us; the launch traced here: 188 us
  waiting for transfers between devices  68 us (36%)
  blocking collectives  52.7 us (28%)
  starting transfers between devices  18.2 us (10%)
  matrix products  18 us (10%)
  between operations  14.8 us (8%)
  other arithmetic  12.3 us (7%)
  local copies, waits for them, and re-layouts  3.92 us (2%)
    all_to_all x1, waiting for transfers between devices, per_device(): lax.all_to_all(send.reshape(N_LIB, 48, bin_count), 'lib', 0, 0)  58.3 us
    unnamed x1, blocking collectives  25.1 us
    all_gather x1, blocking collectives, per_device(): query_block = lax.all_gather(queries, 'query', axis=0, tiled=True)  16.1 us
    all_to_all x1, starting transfers between devices, per_device(): lax.all_to_all(send.reshape(N_LIB, 48, bin_count), 'lib', 0, 0)  11 us
    all_to_all x1, waiting for transfers between devices, per_device(): lax.all_to_all(send_time.reshape(N_LIB, 48), 'lib', 0, 0)  9.69 us
    all_to_all x1, starting transfers between devices, per_device(): lax.all_to_all(send_time.reshape(N_LIB, 48), 'lib', 0, 0)  7.13 us
    dot_general x1, matrix products, per_device(): jnp.dot(pick, library, preferred_element_type=jnp.float32)  7.11 us
    psum x1, blocking collectives, per_device(): total_all, time_all = lax.psum((total_part, time_part), 'query')  5.78 us
  transfers between devices with their start and end apart: 3, of which 2 were waited for; matrix products, arithmetic and copies ran while one was open for 3% of the time, Pallas kernels for 0%

profile of v1, /device:TPU:0, one launch (start us, length us, event | category | flops | bytes accessed | tf_op | source)
XLA Modules:
  0.0 187.8 jit_solution(15114478839216429072)
XLA Ops:
  7.2 0.0 copy-start
  7.2 1.2 convert_reduce_fusion
  8.4 0.7 multiply_add_fusion
  9.1 7.1 %convolution_convert_fusion = bf16[1536,2048]{1,0:T(8,128)(2,1)} fusion(bf16[768,2048]{1,0:T(8,128)(2,1)S(1)} %copy-done, s32[768]{0:T(1024)S(1)} %multiply_add_fusion, s32[1536]{0:T(1024)S(1)} %fusion.18), kind=kOutput, calls=%fused_computation.1 | convolution fusion | flops 4836163584 | bytes 9446400 | tf_op jit(solution)/shard_map/dot_general | solution.py:30
  16.2 11.0 %all-to-all-start = ((bf16[32,48,2048]{2,1,0:T(8,128)(2,1)}), bf16[32,48,2048]{2,1,0:T(8,128)(2,1)}, u32[]{:S(2)}, u32[]{:S(2)}) async-start(bf16[32,48,2048]{2,1,0:T(8,128)(2,1)} %bitcast.17), calls=%async_computation | async-start | bytes 12582912 | tf_op jit(solution)/shard_map/all_to_all | solution.py:32
  27.2 0.0 reduce-scatter.2.cloned.1.call-start
  27.3 0.6 dynamic-slice
  28.6 0.2 dynamic-update-slice
  28.8 25.1 %all-reduce = s32[128]{0:T(128)S(1)} all-reduce(s32[128]{0:T(128)S(1)} %dynamic-update-slice), channel_id=1, replica_groups=mesh['query'=4,'lib'=32] {'query'}, use_global_device_ids=true, to_apply=%add | all-reduce | flops 128 | bytes 1024
  54.0 16.1 %all_gather.7 = bf16[128,2048]{1,0:T(8,128)(2,1)S(1)} all-gather(bf16[32,2048]{1,0:T(8,128)(2,1)S(1)} %copy-done.2), channel_id=1, replica_groups=mesh['query'=4,'lib'=32] {'query'}, dimensions={0}, use_global_device_ids=true | all-gather | bytes 655360 | tf_op jit(solution)/shard_map/all_gather | solution.py:34
  70.1 0.8 copy-done.1
  71.0 0.2 multiply_reduce_fusion.1
  71.2 58.3 %all-to-all-done = bf16[32,48,2048]{2,1,0:T(8,128)(2,1)} async-done(((bf16[32,48,2048]{2,1,0:T(8,128)(2,1)}), bf16[32,48,2048]{2,1,0:T(8,128)(2,1)}, u32[]{:S(2)}, u32[]{:S(2)}) %all-to-all-start) | async-done | bytes 6291488 | tf_op jit(solution)/shard_map/all_to_all | solution.py:32
  129.4 4.1 %multiply_reduce_fusion = f32[32,48]{1,0:T(8,128)S(1)} fusion(bf16[32,48,2048]{2,1,0:T(8,128)(2,1)} %all-to-all-done), kind=kLoop, calls=%fused_computation | loop fusion | flops 9435648 | bytes 6297600 | tf_op jit(solution)/shard_map/reduce_sum | solution.py:12
  133.5 0.1 rsqrt.19
  133.6 5.0 %fusion.26 = (f32[128]{0:T(128)S(1)}, f32[128,1536]{0,1:T(8,128)}) fusion(f32[1536]{0:T(1024)S(1)} %rsqrt.19, f32[128]{0:T(128)S(1)} %rsqrt_multiply_fusion, bf16[1536,2048]{1,0:T(8,128)(2,1)} %bitcast.2, bf16[128,2048]{1,0:T(8,128)(2,1)} %copy-done.1, pred[1536]{0:T(1024)(128)(4,1)S(1)} %get-tuple-element.11, pred[1536]{0:T(1024)(128)(4,1)S(1)} %get-tuple-element.12, ...), kind=kOutput, calls=%fused_computation.50 | convolution fusion | flops 807075712 | bytes 7619072 | tf_op jit(solution)/shard_map/dot_general | solution.py:37
  138.6 5.6 %pmax.7 = f32[128]{0:T(128)S(1)} all-reduce(f32[128]{0:T(128)S(1)} %get-tuple-element.9), channel_id=1, replica_groups=mesh['query'=4,'lib'=32] {'query'}, use_global_device_ids=true, to_apply=%region_4.5 | all-reduce | flops 128 | bytes 1024 | tf_op jit(solution)/shard_map/pmax | solution.py:42
  144.2 1.9 convert_reduce_fusion.1
  146.1 4.8 %fusion.27 = f32[128,2048]{1,0:T(8,128)} fusion(bf16[128,1536]{0,1:T(8,128)(2,1)S(1)} %get-tuple-element.8, bf16[1536,2048]{1,0:T(8,128)(2,1)} %bitcast.2), kind=kOutput, calls=%fused_computation.51 | convolution fusion | flops 805306368 | bytes 7733248 | tf_op jit(solution)/shard_map/dot_general | solution.py:45
  150.9 0.0 reduce-scatter.2.cloned.1.call-update
  150.9 0.7 reshape.98
  151.6 0.9 fusion.11
  152.5 0.7 all_to_all.12
  153.2 7.1 %all-to-all-start.1 = ((bf16[32,1,48]{2,1,0:T(2,128)(2,1)}), bf16[32,1,48]{2,1,0:T(2,128)(2,1)S(1)}, u32[]{:S(2)}, u32[]{:S(2)}) async-start(bf16[32,1,48]{2,1,0:T(2,128)(2,1)} %all_to_all.12), calls=%async_computation.2 | async-start | bytes 32768 | tf_op jit(solution)/shard_map/all_to_all | solution.py:33
  160.3 9.7 %all-to-all-done.1 = bf16[32,1,48]{2,1,0:T(2,128)(2,1)S(1)} async-done(((bf16[32,1,48]{2,1,0:T(2,128)(2,1)}), bf16[32,1,48]{2,1,0:T(2,128)(2,1)S(1)}, u32[]{:S(2)}, u32[]{:S(2)}) %all-to-all-start.1) | async-done | bytes 3104 | tf_op jit(solution)/shard_map/all_to_all | solution.py:33
  170.0 0.7 reduce.2
  170.7 0.8 reshape.100
  171.5 0.2 convolution_bitcast_fusion
  171.6 5.8 %all-reduce.1 = (f32[128]{0:T(128)S(1)}, f32[128]{0:T(128)S(1)}) all-reduce(f32[128]{0:T(128)} %get-tuple-element.7, f32[128]{0:T(128)S(1)} %convolution_bitcast_fusion), channel_id=1, replica_groups=mesh['query'=4,'lib'=32] {'query'}, use_global_device_ids=true, to_apply=%region_7.8 | all-reduce | flops 256 | bytes 2048 | tf_op jit(solution)/shard_map/psum | solution.py:47
  177.4 1.3 log_add_fusion
  178.7 0.6 dynamic-slice_divide_fusion
  179.3 1.7 divide_convert_fusion
  (17 shorter events, 0.1 us)
Async XLA Ops:
  7.2 1.9 %copy-start = (bf16[768,2048]{1,0:T(8,128)(2,1)S(1)}, bf16[768,2048]{1,0:T(8,128)(2,1)}, u32[]{:S(2)}) copy-start(bf16[768,2048]{1,0:T(8,128)(2,1)} %param.7) | copy-start | bytes 9437188
  16.2 11.1 %copy-start.5 = (u32[128]{0:T(128)S(1)}, u32[128]{0:T(128)}, u32[]{:S(2)}) copy-start(u32[128]{0:T(128)} %constant.75) | copy-start | bytes 1540
  16.2 12.3 %copy-start.4 = (s32[32]{0:T(128)S(1)}, s32[32]{0:T(128)}, u32[]{:S(2)}) copy-start(s32[32]{0:T(128)} %param.6) | copy-start | bytes 388
  16.2 37.8 %copy-start.2 = (bf16[32,2048]{1,0:T(8,128)(2,1)S(1)}, bf16[32,2048]{1,0:T(8,128)(2,1)}, u32[]{:S(2)}) copy-start(bf16[32,2048]{1,0:T(8,128)(2,1)} %param.5) | copy-start | bytes 393220
  16.2 113.2 %all-to-all-start = ((bf16[32,48,2048]{2,1,0:T(8,128)(2,1)}), bf16[32,48,2048]{2,1,0:T(8,128)(2,1)}, u32[]{:S(2)}, u32[]{:S(2)}) async-start(bf16[32,48,2048]{2,1,0:T(8,128)(2,1)} %bitcast.17), calls=%async_computation | async-start | bytes 12582912 | tf_op jit(solution)/shard_map/all_to_all | solution.py:32
  27.2 152.0 %reduce-scatter.2.cloned.1.call-start = ((), (), s32[]{:S(2)}) async-start(), calls=%async_computation.3 | async-start | bytes 1310720 | tf_op jit(solution)/shard_map/reduce_scatter | solution.py:48
  70.1 0.8 copy-start.1
  144.2 6.7 %copy-start.3 = (f32[128]{0:T(128)}, f32[128]{0:T(128)S(1)}, u32[]{:S(2)}) copy-start(f32[128]{0:T(128)S(1)} %pmax.7) | copy-start | bytes 1540
  153.2 16.8 %all-to-all-start.1 = ((bf16[32,1,48]{2,1,0:T(2,128)(2,1)}), bf16[32,1,48]{2,1,0:T(2,128)(2,1)S(1)}, u32[]{:S(2)}, u32[]{:S(2)}) async-start(bf16[32,1,48]{2,1,0:T(2,128)(2,1)} %all_to_all.12), calls=%async_computation.2 | async-start | bytes 32768 | tf_op jit(solution)/shard_map/all_to_all | solution.py:33
Sparse Core Ops, SparseCore 0:
  151.0 19.4 reduce-scatter.1
